TPU v7x, 32 devices: a whole 2x2x4 slice. The times are simulated.
32 devices in a mesh: expert: 8 (over y, x, core), tensor: 4 (over z).
Axes of the slice: x: 2, y: 2, z: 4, core: 2. Of those that a mesh axis runs over, the one named last changes fastest.
Arguments:
- inputs: float32 [7880, 512], P('expert'), may hold values from -6 to 6
- cotangent: float32 [7880, 512], P('expert'), may hold values from -6 to 6
- routes: int32 [2, 7880, 2], P(None, 'expert'), may hold values from 0 to 7, all different within a row
- priority: int32 [2, 7880], P(None, 'expert'), may hold values from 0 to 984, as said below
- attend_in: float32 [2, 3, 512, 512], P(None, None, 'expert', 'tensor'), may hold values from -0.375 to 0.375
- attend_out: float32 [2, 512, 512], P(None, 'tensor', 'expert'), may hold values from -1.5 to 1.5
- router: float32 [2, 512, 8], P(None, None, 'expert'), may hold values from -0.1875 to 0.1875
- norm_gains: float32 [2, 2, 512], P(None, None, 'expert'), may hold values from 0.25 to 1.75
- expert_in: float32 [2, 8, 512, 2048], P(None, 'expert', None, 'tensor'), may hold values from -0.25 to 0.25
- expert_out: float32 [2, 8, 2048, 512], P(None, 'expert', 'tensor'), may hold values from -0.5 to 0.5
Outputs:
- outputs: float32 [7880, 512], P('expert')
- input_grad: float32 [7880, 512], P('expert')
- attend_in_grad: float32 [2, 3, 512, 512], P(None, None, 'expert', 'tensor')
- attend_out_grad: float32 [2, 512, 512], P(None, 'tensor', 'expert')
- router_grad: float32 [2, 512, 8], P(None, None, 'expert')
- gains_grad: float32 [2, 2, 512], P(None, None, 'expert')
- expert_in_grad: float32 [2, 8, 512, 2048], P(None, 'expert', None, 'tensor')
- expert_out_grad: float32 [2, 8, 2048, 512], P(None, 'expert', 'tensor')
Inputs may be any that keep to these rules, and one draw needn't show every extreme that they name: `routes`: in each block each token names two different experts, and every expert is named by some token. `priority`: in each block, the values within each device's 985 tokens are a permutation.
All inputs are finite; a program needn't handle non-finite values.
Results may differ from a plain program's by a relative error of at most 0.025.
The roundings to bfloat16 on the way count: a program that leaves them out, or rounds other values in their place, can miss the bound.
Values may be sent and summed in bfloat16 or wider, within the bound.
A program may use at most 192 MiB of HBM per device.

v0:
```python
import jax
import jax.numpy as jnp
from jax import lax
from jax.sharding import PartitionSpec as P

HEAD_DIM = 64
SEQ = 197


def norm_rows(rows_in, gain_row):
    centred = rows_in - jnp.mean(rows_in, axis=-1, keepdims=True)
    spread = jnp.mean(centred * centred, axis=-1, keepdims=True)
    return centred * lax.rsqrt(spread + 1e-06) * gain_row


def gelu_exact(rows_in):
    return 0.5 * rows_in * (1.0 + lax.erf(rows_in * 0.7071067811865476))


def contract_rows(left_side, right_side):
    return lax.dot_general(
        left_side, right_side, (((0,), (0,)), ((), ())), preferred_element_type=jnp.float32
    )


def contract_last(left_side, right_side):
    return lax.dot_general(
        left_side, right_side, (((1,), (1,)), ((), ())), preferred_element_type=jnp.float32
    )


def exchange(rows):
    return lax.all_to_all(rows, "expert", split_axis=0, concat_axis=0, tiled=True)


def own_part(rows, width, axis=1):
    return lax.dynamic_slice_in_dim(rows, lax.axis_index("tensor") * width, width, axis=axis)


def slot_plan(chosen, rank_rows, experts, capacity):
    columns = lax.broadcasted_iota(jnp.int32, (1, experts), 1)
    first_hot = (chosen[:, 0:1] == columns).astype(jnp.bfloat16)
    second = (chosen[:, 1:2] == columns).astype(jnp.bfloat16)
    earlier = (rank_rows[None, :] < rank_rows[:, None]).astype(jnp.bfloat16)
    count_first = jnp.dot(earlier, first_hot, preferred_element_type=jnp.float32)
    count_second = jnp.dot(earlier, second, preferred_element_type=jnp.float32)
    first_f = first_hot.astype(jnp.float32)
    second_f = second.astype(jnp.float32)
    filled = jnp.sum(first_f, axis=0, keepdims=True)
    slot_first = jnp.sum(count_first * first_f, axis=1)
    slot_second = jnp.sum((filled + count_second) * second_f, axis=1)
    slot_nums = jnp.stack([slot_first, slot_second], axis=1).astype(jnp.int32)
    target = jnp.where(slot_nums < capacity, chosen * capacity + slot_nums, experts * capacity)
    return (target, first_f, second_f)


def local(
    inputs,
    cotangent,
    routes,
    priority,
    attend_in,
    attend_out,
    router,
    norm_gains,
    expert_in,
    expert_out,
):
    experts = lax.axis_size("expert")
    tokens = inputs.shape[0]
    model_width = inputs.shape[1]
    images = tokens // SEQ
    head_cols = attend_in.shape[3]
    hidden_cols = expert_in.shape[3]
    local_heads = head_cols * lax.axis_size("tensor") // HEAD_DIM
    layers = attend_in.shape[0]
    capacity = max(2, (10 * tokens + 4 * experts - 1) // (4 * experts))
    slots_all = experts * capacity
    score_scale = HEAD_DIM ** (-0.5)
    layer_ids = range(layers)
    gains_full = lax.all_gather(norm_gains.astype(jnp.bfloat16), "expert", axis=2, tiled=True)
    router_full = lax.all_gather(router.astype(jnp.bfloat16), "expert", axis=2, tiled=True)
    in_full = []
    out_full = []
    win_full = []
    wout_full = []
    for layer_index in layer_ids:
        in_part = lax.all_gather(
            attend_in[layer_index].astype(jnp.bfloat16), "tensor", axis=2, tiled=True
        )
        in_full.append(lax.all_gather(in_part, "expert", axis=1, tiled=True))
        out_part = lax.all_gather(
            attend_out[layer_index].astype(jnp.bfloat16), "tensor", axis=0, tiled=True
        )
        out_full.append(lax.all_gather(out_part, "expert", axis=1, tiled=True))
        win_full.append(
            lax.all_gather(
                expert_in[layer_index, 0].astype(jnp.bfloat16), "tensor", axis=1, tiled=True
            )
        )
        wout_full.append(
            lax.all_gather(
                expert_out[layer_index, 0].astype(jnp.bfloat16), "tensor", axis=0, tiled=True
            )
        )
    slot_ids = lax.broadcasted_iota(jnp.int32, (1, slots_all), 1)
    stream = inputs
    stash_list = []
    for layer_index in range(layers):
        gains_now = gains_full[layer_index].astype(jnp.float32)
        normed = norm_rows(stream, gains_now[0]).astype(jnp.bfloat16)
        project = in_full[layer_index]
        triple = jnp.einsum(
            "td,jdh->jth", normed, project, preferred_element_type=jnp.float32
        ).astype(jnp.bfloat16)
        shaped = triple.reshape(3, images, SEQ, local_heads, HEAD_DIM)
        scores = (
            jnp.einsum("iqhd,ikhd->ihqk", shaped[0], shaped[1], preferred_element_type=jnp.float32)
            * score_scale
        )
        log_total = jax.nn.logsumexp(scores, axis=-1, keepdims=True)
        attention = jnp.exp(scores - log_total).astype(jnp.bfloat16)
        mixed_heads = (
            jnp.einsum("ihqk,ikhd->iqhd", attention, shaped[2], preferred_element_type=jnp.float32)
            .astype(jnp.bfloat16)
            .reshape(tokens, -1)
        )
        middle = stream + jnp.dot(
            mixed_heads, out_full[layer_index], preferred_element_type=jnp.float32
        )
        normed_two = norm_rows(middle, gains_now[1]).astype(jnp.bfloat16)
        logits = jnp.dot(normed_two, router_full[layer_index], preferred_element_type=jnp.float32)
        probs_all = jax.nn.softmax(logits, axis=-1)
        chosen = routes[layer_index]
        target, first_f, second_f = slot_plan(chosen, priority[layer_index], experts, capacity)
        gate_values = jnp.stack(
            [jnp.sum(probs_all * first_f, axis=1), jnp.sum(probs_all * second_f, axis=1)], axis=1
        )
        pick_first = (target[:, 0:1] == slot_ids).astype(jnp.bfloat16)
        pick_second = (target[:, 1:2] == slot_ids).astype(jnp.bfloat16)
        pick_both = pick_first + pick_second
        dispatched = contract_rows(pick_both, normed_two).astype(jnp.bfloat16)
        arrived = exchange(dispatched.reshape(experts, capacity, model_width)).reshape(
            slots_all, model_width
        )
        before = jnp.dot(arrived, win_full[layer_index], preferred_element_type=jnp.float32)
        hidden = gelu_exact(before).astype(jnp.bfloat16)
        expert_rows = jnp.dot(
            hidden, wout_full[layer_index], preferred_element_type=jnp.float32
        ).astype(jnp.bfloat16)
        returned = exchange(expert_rows.reshape(experts, capacity, model_width)).reshape(
            slots_all, model_width
        )
        rows_first = jnp.dot(pick_first, returned, preferred_element_type=jnp.float32)
        rows_second = jnp.dot(pick_second, returned, preferred_element_type=jnp.float32)
        output = middle + gate_values[:, 0:1] * rows_first + gate_values[:, 1:2] * rows_second
        stash_list.append(
            (
                stream,
                gains_now,
                normed,
                shaped,
                log_total,
                mixed_heads,
                middle,
                normed_two,
                probs_all,
                gate_values,
                target,
                first_f,
                second_f,
                pick_first,
                pick_second,
                pick_both,
                arrived,
                rows_first,
                rows_second,
            )
        )
        stream = output
    upstream = cotangent
    grads_in, grads_out, grads_router, grads_gain, grads_win, grads_wout = ([], [], [], [], [], [])
    for layer_index in reversed(range(layers)):
        (
            stream_in,
            gains_now,
            normed,
            shaped,
            log_total,
            mixed_heads,
            middle,
            normed_two,
            probs_all,
            gate_values,
            target,
            first_f,
            second_f,
            pick_first,
            pick_second,
            pick_both,
            arrived,
            rows_first,
            rows_second,
        ) = stash_list[layer_index]
        gate_first = jnp.sum(upstream * rows_first, axis=1)
        gate_second = jnp.sum(upstream * rows_second, axis=1)
        scaled_first = (gate_values[:, 0:1] * upstream).astype(jnp.bfloat16)
        scaled_second = (gate_values[:, 1:2] * upstream).astype(jnp.bfloat16)
        grad_slots = (
            contract_rows(pick_first, scaled_first) + contract_rows(pick_second, scaled_second)
        ).astype(jnp.bfloat16)
        grad_arrived = exchange(grad_slots.reshape(experts, capacity, model_width)).reshape(
            slots_all, model_width
        )
        before = jnp.dot(arrived, win_full[layer_index], preferred_element_type=jnp.float32)
        hidden = gelu_exact(before).astype(jnp.bfloat16)
        grads_wout.append(contract_rows(own_part(hidden, hidden_cols), grad_arrived))
        grad_hidden = contract_last(grad_arrived, wout_full[layer_index])
        grad_before = jax.vjp(gelu_exact, before)[1](grad_hidden)[0].astype(jnp.bfloat16)
        grads_win.append(contract_rows(arrived, own_part(grad_before, hidden_cols)))
        grad_rows = contract_last(grad_before, win_full[layer_index]).astype(jnp.bfloat16)
        grad_dispatched = exchange(grad_rows.reshape(experts, capacity, model_width)).reshape(
            slots_all, model_width
        )
        grad_normed = jnp.dot(pick_both, grad_dispatched, preferred_element_type=jnp.float32)
        grad_probs = first_f * gate_first[:, None] + second_f * gate_second[:, None]
        grad_logits = (
            probs_all * (grad_probs - jnp.sum(probs_all * grad_probs, axis=1, keepdims=True))
        ).astype(jnp.bfloat16)
        grads_router.append(contract_rows(normed_two, grad_logits))
        grad_normed = grad_normed + contract_last(grad_logits, router_full[layer_index])
        norm_back = jax.vjp(norm_rows, middle, gains_now[1])[1](grad_normed)
        grad_middle = upstream + norm_back[0]
        grad_branch = grad_middle.astype(jnp.bfloat16)
        grads_out.append(contract_rows(own_part(mixed_heads, head_cols), grad_branch))
        grad_mixed = (
            contract_last(grad_branch, out_full[layer_index])
            .astype(jnp.bfloat16)
            .reshape(images, SEQ, local_heads, HEAD_DIM)
        )
        scores = (
            jnp.einsum("iqhd,ikhd->ihqk", shaped[0], shaped[1], preferred_element_type=jnp.float32)
            * score_scale
        )
        attention_f = jnp.exp(scores - log_total)
        attention = attention_f.astype(jnp.bfloat16)
        grad_value = jnp.einsum(
            "ihqk,iqhd->ikhd", attention, grad_mixed, preferred_element_type=jnp.float32
        ).astype(jnp.bfloat16)
        grad_attention = jnp.einsum(
            "iqhd,ikhd->ihqk", grad_mixed, shaped[2], preferred_element_type=jnp.float32
        )
        grad_scores = (
            attention_f
            * (grad_attention - jnp.sum(attention_f * grad_attention, axis=-1, keepdims=True))
        ).astype(jnp.bfloat16)
        grad_query = (
            jnp.einsum(
                "ihqk,ikhd->iqhd", grad_scores, shaped[1], preferred_element_type=jnp.float32
            )
            * score_scale
        ).astype(jnp.bfloat16)
        grad_key = (
            jnp.einsum(
                "ihqk,iqhd->ikhd", grad_scores, shaped[0], preferred_element_type=jnp.float32
            )
            * score_scale
        ).astype(jnp.bfloat16)
        grad_triple = jnp.stack([grad_query, grad_key, grad_value]).reshape(3, tokens, -1)
        grads_in.append(
            jnp.einsum(
                "td,jth->jdh",
                normed,
                own_part(grad_triple, head_cols, 2),
                preferred_element_type=jnp.float32,
            )
        )
        project = in_full[layer_index]
        grad_normed_one = jnp.einsum(
            "jth,jdh->td", grad_triple, project, preferred_element_type=jnp.float32
        )
        norm_back_one = jax.vjp(norm_rows, stream_in, gains_now[0])[1](grad_normed_one)
        grads_gain.append(jnp.stack([norm_back_one[1], norm_back[1]]))
        upstream = grad_middle + norm_back_one[0]
    in_grad_all = jnp.stack(grads_in[::-1])
    out_grad_all = jnp.stack(grads_out[::-1])
    router_grad_all = jnp.stack(grads_router[::-1])
    gain_grad_all = jnp.stack(grads_gain[::-1])
    reduced = (
        lax.psum_scatter(in_grad_all, "expert", scatter_dimension=2, tiled=True),
        lax.psum_scatter(out_grad_all, "expert", scatter_dimension=2, tiled=True),
        lax.psum_scatter(router_grad_all, "expert", scatter_dimension=2, tiled=True),
        lax.psum_scatter(gain_grad_all, "expert", scatter_dimension=2, tiled=True),
    )
    win_grad_all = jnp.stack(grads_win[::-1])[:, None]
    wout_grad_all = jnp.stack(grads_wout[::-1])[:, None]
    return (
        stream,
        upstream,
        reduced[0],
        reduced[1],
        reduced[2],
        reduced[3],
        win_grad_all,
        wout_grad_all,
    )


def solution(mesh):
    placed = (
        P("expert", None),
        P("expert", None),
        P(None, "expert", None),
        P(None, "expert"),
        P(None, None, "expert", "tensor"),
        P(None, "tensor", "expert"),
        P(None, None, "expert"),
        P(None, None, "expert"),
        P(None, "expert", None, "tensor"),
        P(None, "expert", "tensor", None),
    )
    return jax.shard_map(
        local,
        mesh=mesh,
        in_specs=placed,
        out_specs=(
            P("expert", None),
            P("expert", None),
            P(None, None, "expert", "tensor"),
            P(None, "tensor", "expert"),
            P(None, None, "expert"),
            P(None, None, "expert"),
            P(None, "expert", None, "tensor"),
            P(None, "expert", "tensor", None),
        ),
        check_vma=False,
    )
```

profile of v0, /device:TPU:0, one launch (start us, length us, event | category | flops | bytes accessed | tf_op | source)
XLA Modules:
  0.0 926.4 jit_solution(8189973012302681919)
XLA Ops:
  8.2 14.9 %all-gather = bf16[1,3,64,512]{3,2,1,0:T(8,128)(2,1)} all-gather(bf16[1,3,64,128]{3,2,1,0:T(8,128)(2,1)S(1)} %get-tuple-element.97), channel_id=2, replica_groups=mesh['expert'=8,'tensor'=4] {'tensor'}, dimensions={3}, use_global_device_ids=true | all-gather | bytes 245760 | tf_op jit(solution)/shard_map/all_gather | solution.py:88
  30.4 9.6 %all_gather.42 = bf16[2,2,512]{1,0,2:T(2,128)(2,1)S(1)} all-gather(bf16[2,2,64]{1,0,2:T(2,128)(2,1)S(1)} %copy.168), channel_id=1, replica_groups=mesh['expert'=8,'tensor'=4] {'expert'}, dimensions={2}, use_global_device_ids=true | all-gather | bytes 4608 | tf_op jit(solution)/shard_map/all_gather | solution.py:81
  43.8 12.0 %all-gather.2 = bf16[1,512,64]{1,2,0:T(8,128)(2,1)S(1)} all-gather(bf16[1,128,64]{1,2,0:T(8,128)(2,1)S(1)} %get-tuple-element.99), channel_id=4, replica_groups=mesh['expert'=8,'tensor'=4] {'tensor'}, dimensions={1}, use_global_device_ids=true | all-gather | bytes 81920 | tf_op jit(solution)/shard_map/all_gather | solution.py:92
  55.8 10.5 %all-gather.3 = bf16[1,512,512]{1,2,0:T(8,128)(2,1)} all-gather(bf16[1,512,64]{1,2,0:T(8,128)(2,1)S(1)} %all-gather.2), channel_id=5, replica_groups=mesh['expert'=8,'tensor'=4] {'expert'}, dimensions={2}, use_global_device_ids=true | all-gather | bytes 589824 | tf_op jit(solution)/shard_map/all_gather | solution.py:95
  66.3 8.2 all_gather.47
  137.0 14.4 %all-gather.6 = bf16[1,3,64,512]{3,2,1,0:T(8,128)(2,1)} all-gather(bf16[1,3,64,128]{3,2,1,0:T(8,128)(2,1)S(1)} %get-tuple-element.96), channel_id=8, replica_groups=mesh['expert'=8,'tensor'=4] {'tensor'}, dimensions={3}, use_global_device_ids=true | all-gather | bytes 245760 | tf_op jit(solution)/shard_map/all_gather | solution.py:88
  151.4 19.1 %all-to-all-done = bf16[8,308,512]{2,1,0:T(8,128)(2,1)S(1)} async-done(((bf16[8,308,512]{2,1,0:T(8,128)(2,1)}), bf16[8,308,512]{2,1,0:T(8,128)(2,1)S(1)}, u32[]{:S(2)}, u32[]{:S(2)}) %all-to-all-start) | async-done | bytes 2523168 | tf_op jit(solution)/shard_map/all_to_all | solution.py:33
  172.7 13.4 %multiply_convert_fusion.1 = (bf16[2464,2048]{1,0:T(8,128)(2,1)}, f32[2464,2048]{1,0:T(8,128)}) fusion(bf16[2464,512]{1,0:T(8,128)(2,1)} %reshape.292, bf16[1,1,512,2048]{3,2,1,0:T(8,128)(2,1)} %all-gather.21.cloned.1.call-done), kind=kOutput, calls=%fused_computation.4 | convolution fusion | flops 5192613888 | bytes 34897920 | tf_op jit(solution)/shard_map/dot_general | solution.py:146
  186.1 9.8 %convolution_convert_fusion.3 = bf16[2464,512]{1,0:T(8,128)(2,1)S(1)} fusion(bf16[2464,2048]{1,0:T(8,128)(2,1)} %get-tuple-element.122, bf16[1,1,2048,512]{3,2,1,0:T(8,128)(2,1)} %all-gather.23.cloned.1.call-done), kind=kOutput, calls=%fused_computation.71 | convolution fusion | flops 5168644096 | bytes 14712832 | tf_op jit(solution)/shard_map/dot_general | solution.py:148
  202.4 12.1 %all-gather.8 = bf16[1,512,64]{1,2,0:T(8,128)(2,1)S(1)} all-gather(bf16[1,128,64]{1,2,0:T(8,128)(2,1)S(1)} %get-tuple-element.98), channel_id=10, replica_groups=mesh['expert'=8,'tensor'=4] {'tensor'}, dimensions={1}, use_global_device_ids=true | all-gather | bytes 81920 | tf_op jit(solution)/shard_map/all_gather | solution.py:92
  214.5 23.9 %all-gather.9 = bf16[1,512,512]{1,2,0:T(8,128)(2,1)} all-gather(bf16[1,512,64]{1,2,0:T(8,128)(2,1)S(1)} %all-gather.8), channel_id=11, replica_groups=mesh['expert'=8,'tensor'=4] {'expert'}, dimensions={2}, use_global_device_ids=true | all-gather | bytes 589824 | tf_op jit(solution)/shard_map/all_gather | solution.py:95
  308.4 31.0 %all-to-all-done.2 = bf16[8,308,512]{2,1,0:T(8,128)(2,1)} async-done(((bf16[8,308,512]{2,1,0:T(8,128)(2,1)}), bf16[8,308,512]{2,1,0:T(8,128)(2,1)}, u32[]{:S(2)}, u32[]{:S(2)}) %all-to-all-start.2) | async-done | bytes 2523168 | tf_op jit(solution)/shard_map/all_to_all | solution.py:33
  343.5 13.5 %multiply_convert_fusion = (bf16[2464,2048]{1,0:T(8,128)(2,1)}, f32[2464,2048]{1,0:T(8,128)}) fusion(bf16[2464,512]{1,0:T(8,128)(2,1)} %reshape.297, bf16[1,1,512,2048]{3,2,1,0:T(8,128)(2,1)} %all-gather.27.cloned.1.call-done), kind=kOutput, calls=%fused_computation.2 | convolution fusion | flops 5192613888 | bytes 34897920 | tf_op jit(solution)/shard_map/dot_general | solution.py:146
  357.0 10.9 %convolution_convert_fusion.2 = bf16[2464,512]{1,0:T(8,128)(2,1)} fusion(bf16[2464,2048]{1,0:T(8,128)(2,1)} %get-tuple-element.129, bf16[1,1,2048,512]{3,2,1,0:T(8,128)(2,1)} %all-gather.29.cloned.1.call-done), kind=kOutput, calls=%fused_computation.70 | convolution fusion | flops 5168644096 | bytes 14712832 | tf_op jit(solution)/shard_map/dot_general | solution.py:148
  378.2 29.9 %all-to-all-done.3 = bf16[8,308,512]{2,1,0:T(8,128)(2,1)} async-done(((bf16[8,308,512]{2,1,0:T(8,128)(2,1)}), bf16[8,308,512]{2,1,0:T(8,128)(2,1)}, u32[]{:S(2)}, u32[]{:S(2)}) %all-to-all-start.3) | async-done | bytes 2523168 | tf_op jit(solution)/shard_map/all_to_all | solution.py:33
  435.5 35.9 %all_to_all.40 = bf16[8,308,512]{2,1,0:T(8,128)(2,1)} all-to-all(bf16[8,308,512]{2,1,0:T(8,128)(2,1)} %reshape.300), channel_id=1, replica_groups=mesh['expert'=8,'tensor'=4] {'expert'}, dimensions={0} | all-to-all | bytes 5046272 | tf_op jit(solution)/shard_map/all_to_all | solution.py:33
  475.6 15.1 %add_convert_fusion.1 = bf16[2464,2048]{1,0:T(8,128)(2,1)S(1)} fusion(f32[2464,2048]{1,0:T(8,128)} %get-tuple-element.130, bf16[2464,512]{1,0:T(8,128)(2,1)} %reshape.301, bf16[1,1,2048,512]{3,2,1,0:T(8,128)(2,1)} %all-gather.29.cloned.1.call-done), kind=kOutput, calls=%fused_computation.1 | convolution fusion | flops 5232984064 | bytes 34897920 | tf_op jit(solution)/shard_map/dot_general | solution.py:27
  510.4 31.5 %all-to-all-done.5 = bf16[8,308,512]{2,1,0:T(8,128)(2,1)} async-done(((bf16[8,308,512]{2,1,0:T(8,128)(2,1)}), bf16[8,308,512]{2,1,0:T(8,128)(2,1)}, u32[]{:S(2)}, u32[]{:S(2)}) %all-to-all-start.5) | async-done | bytes 2523168 | tf_op jit(solution)/shard_map/all_to_all | solution.py:33
  633.4 20.5 %all-to-all-done.6 = bf16[8,308,512]{2,1,0:T(8,128)(2,1)} async-done(((bf16[8,308,512]{2,1,0:T(8,128)(2,1)}), bf16[8,308,512]{2,1,0:T(8,128)(2,1)}, u32[]{:S(2)}, u32[]{:S(2)}) %all-to-all-start.6) | async-done | bytes 2523168 | tf_op jit(solution)/shard_map/all_to_all | solution.py:33
  658.0 15.2 %add_convert_fusion = bf16[2464,2048]{1,0:T(8,128)(2,1)S(1)} fusion(f32[2464,2048]{1,0:T(8,128)} %get-tuple-element.123, bf16[2464,512]{1,0:T(8,128)(2,1)} %reshape.306, bf16[1,1,2048,512]{3,2,1,0:T(8,128)(2,1)} %all-gather.23.cloned.1.call-done), kind=kOutput, calls=%fused_computation | convolution fusion | flops 5232984064 | bytes 34897920 | tf_op jit(solution)/shard_map/dot_general | solution.py:27
  677.1 7.0 convolution_convert_fusion
  693.2 47.9 %all-reduce.2 = f32[2,512,8]{1,0,2:T(2,128)S(1)} all-reduce(f32[2,512,8]{1,0,2:T(2,128)S(1)} %copy.206), channel_id=16, replica_groups=mesh['expert'=8,'tensor'=4] {'expert'}, use_global_device_ids=true, to_apply=%region_44.45.clone | all-reduce | flops 8192 | bytes 65536
  830.0 20.8 %reduce-scatter.4.cloned.1.call-done = f32[64,4]{1,0:T(8,128)} async-done(((f32[512,4]{1,0:T(8,128)}), f32[64,4]{1,0:T(8,128)}) %reduce-scatter.4.cloned.1.call-update) | async-done | bytes 1040
  852.3 63.7 %all-reduce.6.cloned.1.call-done = (f32[2,3,512,128]{3,0,1,2:T(2,128)}, f32[2,128,512]{1,0,2:T(2,128)}) async-done(((f32[2,3,512,128]{3,0,1,2:T(2,128)}, f32[2,128,512]{1,0,2:T(2,128)}), (f32[2,3,512,128]{3,0,1,2:T(2,128)}, f32[2,128,512]{1,0,2:T(2,128)})) %all-reduce.6.cloned.1.call-update) | async-done | bytes 2097168
  (470 shorter events, 418.1 us)
Async XLA Ops:
  7.2 70.1 %all-gather.19.cloned.1.call-start = ((), (), s32[]{:S(2)}) async-start(), calls=%async_computation.9 | async-start | bytes 1769472 | tf_op jit(solution)/shard_map/all_gather | solution.py:91
  23.1 149.6 %all-gather.21.cloned.1.call-start = ((), (), s32[]{:S(2)}) async-start(), calls=%async_computation.10 | async-start | bytes 2621440 | tf_op jit(solution)/shard_map/all_gather | solution.py:97
  25.9 160.2 %all-gather.23.cloned.1.call-start = ((), (), s32[]{:S(2)}) async-start(), calls=%async_computation.11 | async-start | bytes 2621440 | tf_op jit(solution)/shard_map/all_gather | solution.py:102
  29.2 48.1 %copy-start.76 = (f32[985]{0:T(1024)}, f32[985]{0:T(1024)S(1)}, u32[]{:S(2)}) copy-start(f32[985]{0:T(1024)S(1)} %broadcast_multiply_fusion.3) | copy-start | bytes 11824
  43.8 80.8 %copy-start.92 = (f32[512]{0:T(512)}, f32[512]{0:T(512)S(1)}, u32[]{:S(2)}) copy-start(f32[512]{0:T(512)S(1)} %get-tuple-element.62) | copy-start | bytes 6148
  74.6 50.4 %copy-start.66 = (bf16[1,512,8]{1,0,2:T(2,128)(2,1)}, bf16[1,512,8]{1,0,2:T(2,128)(2,1)S(1)}, u32[]{:S(2)}) copy-start(bf16[1,512,8]{1,0,2:T(2,128)(2,1)S(1)} %get-tuple-element.101) | copy-start | bytes 24580
  74.7 50.8 %copy-start.74 = (s32[985,1]{0,1:T(1,128)}, s32[985,1]{0,1:T(1,128)S(1)}, u32[]{:S(2)}) copy-start(s32[985,1]{0,1:T(1,128)S(1)} %get-tuple-element.143) | copy-start | bytes 11824
  74.7 51.5 %copy-start.72 = (s32[985,1]{0,1:T(1,128)}, s32[985,1]{0,1:T(1,128)S(1)}, u32[]{:S(2)}) copy-start(s32[985,1]{0,1:T(1,128)S(1)} %get-tuple-element.142) | copy-start | bytes 11824
  126.1 122.0 %copy-start.99 = (f32[985]{0:T(1024)}, f32[985]{0:T(1024)S(1)}, u32[]{:S(2)}) copy-start(f32[985]{0:T(1024)S(1)} %get-tuple-element.67) | copy-start | bytes 11824
  126.1 122.0 %copy-start.101 = (f32[985]{0:T(1024)}, f32[985]{0:T(1024)S(1)}, u32[]{:S(2)}) copy-start(f32[985]{0:T(1024)S(1)} %get-tuple-element.68) | copy-start | bytes 11824
  127.0 116.3 %copy-start.104 = (s32[985,1]{0,1:T(1,128)}, s32[985,1]{0,1:T(1,128)S(1)}, u32[]{:S(2)}) copy-start(s32[985,1]{0,1:T(1,128)S(1)} %get-tuple-element.112) | copy-start | bytes 11824
  127.0 121.1 %copy-start.106 = (s32[985,1]{0,1:T(1,128)}, s32[985,1]{0,1:T(1,128)S(1)}, u32[]{:S(2)}) copy-start(s32[985,1]{0,1:T(1,128)S(1)} %get-tuple-element.113) | copy-start | bytes 11824
  133.3 37.2 %all-to-all-start = ((bf16[8,308,512]{2,1,0:T(8,128)(2,1)}), bf16[8,308,512]{2,1,0:T(8,128)(2,1)S(1)}, u32[]{:S(2)}, u32[]{:S(2)}) async-start(bf16[8,308,512]{2,1,0:T(8,128)(2,1)} %reshape.291), calls=%async_computation | async-start | bytes 5111808 | tf_op jit(solution)/shard_map/all_to_all | solution.py:33
  137.0 116.4 %all-gather.25.cloned.1.call-start = ((), (), s32[]{:S(2)}) async-start(), calls=%async_computation.12 | async-start | bytes 1769472 | tf_op jit(solution)/shard_map/all_gather | solution.py:91
  198.1 43.1 %all-to-all-start.1 = ((bf16[8,308,512]{2,1,0:T(8,128)(2,1)}), bf16[8,308,512]{2,1,0:T(8,128)(2,1)S(1)}, u32[]{:S(2)}, u32[]{:S(2)}) async-start(bf16[8,308,512]{2,1,0:T(8,128)(2,1)} %reshape.293), calls=%async_computation.1 | async-start | bytes 5111808 | tf_op jit(solution)/shard_map/all_to_all | solution.py:33
  201.8 141.7 %all-gather.27.cloned.1.call-start = ((), (), s32[]{:S(2)}) async-start(), calls=%async_computation.13 | async-start | bytes 2621440 | tf_op jit(solution)/shard_map/all_gather | solution.py:97
  303.4 36.0 %all-to-all-start.2 = ((bf16[8,308,512]{2,1,0:T(8,128)(2,1)}), bf16[8,308,512]{2,1,0:T(8,128)(2,1)}, u32[]{:S(2)}, u32[]{:S(2)}) async-start(bf16[8,308,512]{2,1,0:T(8,128)(2,1)} %reshape.296), calls=%async_computation.2 | async-start | bytes 5111808 | tf_op jit(solution)/shard_map/all_to_all | solution.py:33
  307.8 49.2 %all-gather.29.cloned.1.call-start = ((), (), s32[]{:S(2)}) async-start(), calls=%async_computation.14 | async-start | bytes 2621440 | tf_op jit(solution)/shard_map/all_gather | solution.py:102
  372.2 36.0 %all-to-all-start.3 = ((bf16[8,308,512]{2,1,0:T(8,128)(2,1)}), bf16[8,308,512]{2,1,0:T(8,128)(2,1)}, u32[]{:S(2)}, u32[]{:S(2)}) async-start(bf16[8,308,512]{2,1,0:T(8,128)(2,1)} %reshape.298), calls=%async_computation.3 | async-start | bytes 5111808 | tf_op jit(solution)/shard_map/all_to_all | solution.py:33
  505.8 36.2 %all-to-all-start.5 = ((bf16[8,308,512]{2,1,0:T(8,128)(2,1)}), bf16[8,308,512]{2,1,0:T(8,128)(2,1)}, u32[]{:S(2)}, u32[]{:S(2)}) async-start(bf16[8,308,512]{2,1,0:T(8,128)(2,1)} %reshape.302), calls=%async_computation.5 | async-start | bytes 5111808 | tf_op jit(solution)/shard_map/all_to_all | solution.py:33
  617.8 36.1 %all-to-all-start.6 = ((bf16[8,308,512]{2,1,0:T(8,128)(2,1)}), bf16[8,308,512]{2,1,0:T(8,128)(2,1)}, u32[]{:S(2)}, u32[]{:S(2)}) async-start(bf16[8,308,512]{2,1,0:T(8,128)(2,1)} %reshape.305), calls=%async_computation.6 | async-start | bytes 5111808 | tf_op jit(solution)/shard_map/all_to_all | solution.py:33
  688.3 70.5 %all-to-all-start.7 = ((bf16[8,308,512]{2,1,0:T(8,128)(2,1)}), bf16[8,308,512]{2,1,0:T(8,128)(2,1)}, u32[]{:S(2)}, u32[]{:S(2)}) async-start(bf16[8,308,512]{2,1,0:T(8,128)(2,1)} %reshape.307), calls=%async_computation.7 | async-start | bytes 5111808 | tf_op jit(solution)/shard_map/all_to_all | solution.py:33
  692.8 158.0 %reduce-scatter.4.cloned.1.call-start = ((), (), s32[]{:S(2)}) async-start(), calls=%async_computation.15 | async-start | bytes 294912
  818.5 97.5 %all-reduce.6.cloned.1.call-start = ((), (), s32[]{:S(2)}) async-start(), calls=%async_computation.16 | async-start | bytes 4194304
  (111 other events, 655.9 us)
Sparse Core Ops, SparseCore 0:
  23.2 26.2 all-gather.18
  51.6 45.6 all-gather.20
  98.9 44.7 all-gather.22
  151.5 26.5 all-gather.24
  203.9 45.2 all-gather.26
  309.9 45.2 all-gather.28
  818.6 32.1 reduce-scatter.3
  854.1 61.8 all-reduce.5
where the time goes:
time: 937 us; the launch traced here: 926 us
  matrix products  244 us (26%)
  waiting for transfers between devices  218 us (23%)
  local copies, waits for them, and re-layouts  196 us (21%)
  blocking collectives  189 us (20%)
  other arithmetic  32 us (3%)
  starting transfers between devices  30.2 us (3%)
  between operations  17.4 us (2%)
    all_to_all x7, waiting for transfers between devices, exchange(): lax.all_to_all(rows, 'expert', split_axis=0, concat_axis=0, tiled=True)  132 us
    unnamed x10, waiting for transfers between devices  85.6 us
    dot_general x14, matrix products, contract_rows(): lax.dot_general(left_side, right_side, (((0,), (0,)), ((), ())), preferre...  49.9 us
    unnamed x1, blocking collectives  47.9 us
    dot_general x8, matrix products, contract_last(): lax.dot_general(left_side, right_side, (((1,), (1,)), ((), ())), preferre...  47.7 us
    all_to_all x1, blocking collectives, exchange(): lax.all_to_all(rows, 'expert', split_axis=0, concat_axis=0, tiled=True)  35.9 us
    unnamed x256, local copies, waits for them, and re-layouts  34.6 us
    all_gather x2, blocking collectives, local(): out_full.append(lax.all_gather(out_part, 'expert', axis=1, tiled=True))  34.4 us
  transfers between devices with their start and end apart: 15, of which 7 were waited for; matrix products, arithmetic and copies ran while one was open for 23% of the time, Pallas kernels for 0%

commit v1 on v0

--- a/solution.py
+++ b/solution.py
@@ -5,6 +5,19 @@
 
 HEAD_DIM = 64
 SEQ = 197
+
+
+def gather_around(shard, axis, dim):
+    ways = lax.axis_size(axis)
+    up = [(d, (d + 1) % ways) for d in range(ways)]
+    down = [(d, (d - 1) % ways) for d in range(ways)]
+    earlier, later = ([shard], [shard])
+    for _ in range(ways // 2):
+        earlier.append(lax.ppermute(earlier[-1], axis, up))
+    for _ in range((ways - 1) // 2):
+        later.append(lax.ppermute(later[-1], axis, down))
+    line = jnp.concatenate([*earlier[::-1], *later[1:]], axis=dim)
+    return jnp.roll(line, (lax.axis_index(axis) - ways // 2) * shard.shape[dim], axis=dim)
 
 
 def norm_rows(rows_in, gain_row):
@@ -88,7 +101,7 @@
         in_part = lax.all_gather(
             attend_in[layer_index].astype(jnp.bfloat16), "tensor", axis=2, tiled=True
         )
-        in_full.append(lax.all_gather(in_part, "expert", axis=1, tiled=True))
+        in_full.append(gather_around(in_part, "expert", 1))
         out_part = lax.all_gather(
             attend_out[layer_index].astype(jnp.bfloat16), "tensor", axis=0, tiled=True
         )

time: 937 us -> 989 us (1.055)
  waiting for transfers between devices: 218 us -> 267 us
  local copies, waits for them, and re-layouts: 196 us -> 208 us
  blocking collectives: 189 us -> 178 us
  starting transfers between devices: 30.2 us -> 41 us
    ppermute x0 -> x14, waiting for transfers between devices: none -> 38.8 us  [the longest x8 35.5 us: gather_around(): earlier.append(lax.ppermute(earlier[-1], axis, up))]
    all_gather x2, blocking collectives: 34.4 us -> 23.2 us  [local(): out_full.append(lax.all_gather(out_part, 'expert', axis=1, tiled=True))]
    all_to_all x7, waiting for transfers between devices: 132 us -> 142 us  [exchange(): lax.all_to_all(rows, 'expert', split_axis=0, concat_axis=0, tiled=True)]
    ppermute x0 -> x14, starting transfers between devices: none -> 9.99 us  [the longest x6 8.56 us: gather_around(): later.append(lax.ppermute(later[-1], axis, down))]
    unnamed x256 -> x306, local copies, waits for them, and re-layouts: 34.6 us -> 39.4 us
    unnamed x10 -> x8, waiting for transfers between devices: 85.6 us -> 84.3 us
  transfers between devices with their start and end apart: 15 -> 27, of which waited for: 7 -> 14; matrix products, arithmetic and copies ran while one was open for 23% -> 21% of each run, Pallas kernels for 0% -> 0%
where the time goes in v1:
time: 989 us; the launch traced here: 979 us
  waiting for transfers between devices  267 us (27%)
  matrix products  236 us (24%)
  local copies, waits for them, and re-layouts  208 us (21%)
  blocking collectives  178 us (18%)
  starting transfers between devices  41 us (4%)
  other arithmetic  32.3 us (3%)
  between operations  17.1 us (2%)
    all_to_all x7, waiting for transfers between devices, exchange(): lax.all_to_all(rows, 'expert', split_axis=0, concat_axis=0, tiled=True)  142 us
    unnamed x8, waiting for transfers between devices  84.3 us
    dot_general x14, matrix products, contract_rows(): lax.dot_general(left_side, right_side, (((0,), (0,)), ((), ())), preferre...  50.7 us
    unnamed x1, blocking collectives  47.9 us
    dot_general x8, matrix products, contract_last(): lax.dot_general(left_side, right_side, (((1,), (1,)), ((), ())), preferre...  47.7 us
    unnamed x306, local copies, waits for them, and re-layouts  39.4 us
    all_to_all x1, blocking collectives, exchange(): lax.all_to_all(rows, 'expert', split_axis=0, concat_axis=0, tiled=True)  35.9 us
    ppermute x8, waiting for transfers between devices, gather_around(): earlier.append(lax.ppermute(earlier[-1], axis, up))  35.5 us
  transfers between devices with their start and end apart: 27, of which 14 were waited for; matrix products, arithmetic and copies ran while one was open for 21% of the time, Pallas kernels for 0%

profile of v1, /device:TPU:0, one launch (start us, length us, event | category | flops | bytes accessed | tf_op | source)
XLA Modules:
  0.0 978.7 jit_solution(7148134744734910825)
XLA Ops:
  8.8 14.2 %all-gather = bf16[1,3,64,512]{3,2,1,0:T(8,128)(2,1)S(1)} all-gather(bf16[1,3,64,128]{3,2,1,0:T(8,128)(2,1)S(1)} %get-tuple-element.98), channel_id=2, replica_groups=mesh['expert'=8,'tensor'=4] {'tensor'}, dimensions={3}, use_global_device_ids=true | all-gather | bytes 245760 | tf_op jit(solution)/shard_map/all_gather | solution.py:101
  26.5 8.9 all_gather.40
  39.4 12.9 %all-gather.1 = bf16[1,512,64]{1,2,0:T(8,128)(2,1)S(1)} all-gather(bf16[1,128,64]{1,2,0:T(8,128)(2,1)S(1)} %get-tuple-element.100), channel_id=3, replica_groups=mesh['expert'=8,'tensor'=4] {'tensor'}, dimensions={1}, use_global_device_ids=true | all-gather | bytes 81920 | tf_op jit(solution)/shard_map/all_gather | solution.py:105
  52.3 9.3 all_gather.37
  79.1 11.2 %all-gather.2 = bf16[1,512,512]{1,2,0:T(8,128)(2,1)} all-gather(bf16[1,512,64]{1,2,0:T(8,128)(2,1)S(1)} %all-gather.1), channel_id=4, replica_groups=mesh['expert'=8,'tensor'=4] {'expert'}, dimensions={2}, use_global_device_ids=true | all-gather | bytes 589824 | tf_op jit(solution)/shard_map/all_gather | solution.py:108
  156.9 28.7 %all-to-all-done = bf16[8,308,512]{2,1,0:T(8,128)(2,1)S(1)} async-done(((bf16[8,308,512]{2,1,0:T(8,128)(2,1)}), bf16[8,308,512]{2,1,0:T(8,128)(2,1)S(1)}, u32[]{:S(2)}, u32[]{:S(2)}) %all-to-all-start) | async-done | bytes 2523168 | tf_op jit(solution)/shard_map/all_to_all | solution.py:46
  187.7 13.4 %multiply_convert_fusion.1 = (bf16[2464,2048]{1,0:T(8,128)(2,1)}, f32[2464,2048]{1,0:T(8,128)}) fusion(bf16[2464,512]{1,0:T(8,128)(2,1)} %reshape.292, bf16[1,1,512,2048]{3,2,1,0:T(8,128)(2,1)} %all-gather.15.cloned.1.call-done), kind=kOutput, calls=%fused_computation.4 | convolution fusion | flops 5192613888 | bytes 34897920 | tf_op jit(solution)/shard_map/dot_general | solution.py:159
  202.9 9.8 %convolution_convert_fusion.3 = bf16[2464,512]{1,0:T(8,128)(2,1)S(1)} fusion(bf16[2464,2048]{1,0:T(8,128)(2,1)} %get-tuple-element.123, bf16[1,1,2048,512]{3,2,1,0:T(8,128)(2,1)} %all-gather.17.cloned.1.call-done), kind=kOutput, calls=%fused_computation.71 | convolution fusion | flops 5168644096 | bytes 14712832 | tf_op jit(solution)/shard_map/dot_general | solution.py:161
  218.8 13.1 %all-gather.5 = bf16[1,3,64,512]{3,2,1,0:T(8,128)(2,1)S(1)} all-gather(bf16[1,3,64,128]{3,2,1,0:T(8,128)(2,1)S(1)} %copy-done.62), channel_id=7, replica_groups=mesh['expert'=8,'tensor'=4] {'tensor'}, dimensions={3}, use_global_device_ids=true | all-gather | bytes 245760 | tf_op jit(solution)/shard_map/all_gather | solution.py:101
  231.9 20.5 %collective-permute-done.7 = bf16[3,64,512]{2,1,0:T(8,128)(2,1)S(1)} collective-permute-done((bf16[3,64,512]{2,1,0:T(8,128)(2,1)S(1)}, bf16[3,64,512]{2,1,0:T(8,128)(2,1)S(1)}, u32[]{:S(2)}, u32[]{:S(2)}) %collective-permute-start.7) | collective-permute-done | bytes 196640 | tf_op jit(solution)/shard_map/ppermute | solution.py:16
  260.8 12.4 %all-gather.6 = bf16[1,512,64]{1,2,0:T(8,128)(2,1)S(1)} all-gather(bf16[1,128,64]{1,2,0:T(8,128)(2,1)S(1)} %copy-done.75), channel_id=8, replica_groups=mesh['expert'=8,'tensor'=4] {'tensor'}, dimensions={1}, use_global_device_ids=true | all-gather | bytes 81920 | tf_op jit(solution)/shard_map/all_gather | solution.py:105
  273.7 12.0 %all-gather.7 = bf16[1,512,512]{1,2,0:T(8,128)(2,1)} all-gather(bf16[1,512,64]{1,2,0:T(8,128)(2,1)S(1)} %all-gather.6), channel_id=9, replica_groups=mesh['expert'=8,'tensor'=4] {'expert'}, dimensions={2}, use_global_device_ids=true | all-gather | bytes 589824 | tf_op jit(solution)/shard_map/all_gather | solution.py:108
  361.7 31.4 %all-to-all-done.2 = bf16[8,308,512]{2,1,0:T(8,128)(2,1)} async-done(((bf16[8,308,512]{2,1,0:T(8,128)(2,1)}), bf16[8,308,512]{2,1,0:T(8,128)(2,1)}, u32[]{:S(2)}, u32[]{:S(2)}) %all-to-all-start.2) | async-done | bytes 2523168 | tf_op jit(solution)/shard_map/all_to_all | solution.py:46
  397.3 13.6 %multiply_convert_fusion = (bf16[2464,2048]{1,0:T(8,128)(2,1)}, f32[2464,2048]{1,0:T(8,128)}) fusion(bf16[2464,512]{1,0:T(8,128)(2,1)} %reshape.297, bf16[1,1,512,2048]{3,2,1,0:T(8,128)(2,1)} %all-gather.19.cloned.1.call-done), kind=kOutput, calls=%fused_computation.2 | convolution fusion | flops 5192613888 | bytes 34897920 | tf_op jit(solution)/shard_map/dot_general | solution.py:159
  411.0 10.9 %convolution_convert_fusion.2 = bf16[2464,512]{1,0:T(8,128)(2,1)} fusion(bf16[2464,2048]{1,0:T(8,128)(2,1)} %get-tuple-element.130, bf16[1,1,2048,512]{3,2,1,0:T(8,128)(2,1)} %all-gather.21.cloned.1.call-done), kind=kOutput, calls=%fused_computation.70 | convolution fusion | flops 5168644096 | bytes 14712832 | tf_op jit(solution)/shard_map/dot_general | solution.py:161
  432.2 29.9 %all-to-all-done.3 = bf16[8,308,512]{2,1,0:T(8,128)(2,1)} async-done(((bf16[8,308,512]{2,1,0:T(8,128)(2,1)}), bf16[8,308,512]{2,1,0:T(8,128)(2,1)}, u32[]{:S(2)}, u32[]{:S(2)}) %all-to-all-start.3) | async-done | bytes 2523168 | tf_op jit(solution)/shard_map/all_to_all | solution.py:46
  489.2 35.9 %all_to_all.40 = bf16[8,308,512]{2,1,0:T(8,128)(2,1)} all-to-all(bf16[8,308,512]{2,1,0:T(8,128)(2,1)} %reshape.300), channel_id=1, replica_groups=mesh['expert'=8,'tensor'=4] {'expert'}, dimensions={0} | all-to-all | bytes 5046272 | tf_op jit(solution)/shard_map/all_to_all | solution.py:46
  529.3 15.1 %add_convert_fusion.1 = bf16[2464,2048]{1,0:T(8,128)(2,1)S(1)} fusion(f32[2464,2048]{1,0:T(8,128)} %get-tuple-element.131, bf16[2464,512]{1,0:T(8,128)(2,1)} %reshape.301, bf16[1,1,2048,512]{3,2,1,0:T(8,128)(2,1)} %all-gather.21.cloned.1.call-done), kind=kOutput, calls=%fused_computation.1 | convolution fusion | flops 5232984064 | bytes 34897920 | tf_op jit(solution)/shard_map/dot_general | solution.py:40
  564.3 31.5 %all-to-all-done.5 = bf16[8,308,512]{2,1,0:T(8,128)(2,1)} async-done(((bf16[8,308,512]{2,1,0:T(8,128)(2,1)}), bf16[8,308,512]{2,1,0:T(8,128)(2,1)}, u32[]{:S(2)}, u32[]{:S(2)}) %all-to-all-start.5) | async-done | bytes 2523168 | tf_op jit(solution)/shard_map/all_to_all | solution.py:46
  688.6 20.5 %all-to-all-done.6 = bf16[8,308,512]{2,1,0:T(8,128)(2,1)} async-done(((bf16[8,308,512]{2,1,0:T(8,128)(2,1)}), bf16[8,308,512]{2,1,0:T(8,128)(2,1)}, u32[]{:S(2)}, u32[]{:S(2)}) %all-to-all-start.6) | async-done | bytes 2523168 | tf_op jit(solution)/shard_map/all_to_all | solution.py:46
  713.2 15.1 %add_convert_fusion = bf16[2464,2048]{1,0:T(8,128)(2,1)S(1)} fusion(f32[2464,2048]{1,0:T(8,128)} %get-tuple-element.124, bf16[2464,512]{1,0:T(8,128)(2,1)} %reshape.306, bf16[1,1,2048,512]{3,2,1,0:T(8,128)(2,1)} %all-gather.17.cloned.1.call-done), kind=kOutput, calls=%fused_computation | convolution fusion | flops 5232984064 | bytes 34897920 | tf_op jit(solution)/shard_map/dot_general | solution.py:40
  748.3 47.9 %all-reduce.2 = f32[2,512,8]{1,0,2:T(2,128)S(1)} all-reduce(f32[2,512,8]{1,0,2:T(2,128)S(1)} %copy.206), channel_id=14, replica_groups=mesh['expert'=8,'tensor'=4] {'expert'}, use_global_device_ids=true, to_apply=%region_44.46.clone | all-reduce | flops 8192 | bytes 65536
  883.3 20.2 %reduce-scatter.4.cloned.1.call-done = f32[64,4]{1,0:T(8,128)} async-done(((f32[512,4]{1,0:T(8,128)}), f32[64,4]{1,0:T(8,128)}) %reduce-scatter.4.cloned.1.call-update) | async-done | bytes 1040
  905.0 63.5 %all-reduce.6.cloned.1.call-done = (f32[2,3,512,128]{3,0,1,2:T(2,128)}, f32[2,128,512]{1,0,2:T(2,128)}) async-done(((f32[2,3,512,128]{3,0,1,2:T(2,128)}, f32[2,128,512]{1,0,2:T(2,128)}), (f32[2,3,512,128]{3,0,1,2:T(2,128)}, f32[2,128,512]{1,0,2:T(2,128)})) %all-reduce.6.cloned.1.call-update) | async-done | bytes 2097168
  (544 shorter events, 459.5 us)
Async XLA Ops:
  7.2 180.6 %all-gather.15.cloned.1.call-start = ((), (), s32[]{:S(2)}) async-start(), calls=%async_computation.9 | async-start | bytes 2621440 | tf_op jit(solution)/shard_map/all_gather | solution.py:110
  23.0 49.2 %collective-permute-start.4 = (bf16[3,64,512]{2,1,0:T(8,128)(2,1)S(1)}, bf16[3,64,512]{2,1,0:T(8,128)(2,1)S(1)}, u32[]{:S(2)}, u32[]{:S(2)}) collective-permute-start(bf16[3,64,512]{2,1,0:T(8,128)(2,1)S(1)} %bitcast.248), channel_id=1, source_target_pairs={{0,28},{4,0},{8,4},{12,8},{16,12},{20,16},{24,20},{28,24},{1,29},{... | collective-permute-start | bytes 589832 | tf_op jit(solution)/shard_map/ppermute | solution.py:18
  23.2 42.5 %collective-permute-start = (bf16[3,64,512]{2,1,0:T(8,128)(2,1)S(1)}, bf16[3,64,512]{2,1,0:T(8,128)(2,1)S(1)}, u32[]{:S(2)}, u32[]{:S(2)}) collective-permute-start(bf16[3,64,512]{2,1,0:T(8,128)(2,1)S(1)} %bitcast.249), channel_id=1, source_target_pairs={{0,4},{4,8},{8,12},{12,16},{16,20},{20,24},{24,28},{28,0},{1,5},{5... | collective-permute-start | bytes 589832 | tf_op jit(solution)/shard_map/ppermute | solution.py:16
  71.6 7.5 collective-permute-start.2
  72.2 21.4 %collective-permute-start.5 = (bf16[3,64,512]{2,1,0:T(8,128)(2,1)S(1)}, bf16[3,64,512]{2,1,0:T(8,128)(2,1)S(1)}, u32[]{:S(2)}, u32[]{:S(2)}) collective-permute-start(bf16[3,64,512]{2,1,0:T(8,128)(2,1)S(1)} %collective-permute-done.4), channel_id=1, source_target_pairs={{0,28},{4,0},{8,4},{12,8},{16,12},{20,16},{24,20},{28,24},{1,29},{... | collective-permute-start | bytes 589832 | tf_op jit(solution)/shard_map/ppermute | solution.py:18
  79.1 16.1 %collective-permute-start.3 = (bf16[3,64,512]{2,1,0:T(8,128)(2,1)S(1)}, bf16[3,64,512]{2,1,0:T(8,128)(2,1)}, u32[]{:S(2)}, u32[]{:S(2)}) collective-permute-start(bf16[3,64,512]{2,1,0:T(8,128)(2,1)S(1)} %collective-permute-done.2), channel_id=1, source_target_pairs={{0,4},{4,8},{8,12},{12,16},{16,20},{20,24},{24,28},{28,0},{1,5},{5... | collective-permute-start | bytes 589832 | tf_op jit(solution)/shard_map/ppermute | solution.py:16
  149.9 35.6 %all-to-all-start = ((bf16[8,308,512]{2,1,0:T(8,128)(2,1)}), bf16[8,308,512]{2,1,0:T(8,128)(2,1)S(1)}, u32[]{:S(2)}, u32[]{:S(2)}) async-start(bf16[8,308,512]{2,1,0:T(8,128)(2,1)} %reshape.291), calls=%async_computation | async-start | bytes 5111808 | tf_op jit(solution)/shard_map/all_to_all | solution.py:46
  154.0 48.9 %all-gather.17.cloned.1.call-start = ((), (), s32[]{:S(2)}) async-start(), calls=%async_computation.10 | async-start | bytes 2621440 | tf_op jit(solution)/shard_map/all_gather | solution.py:115
  214.9 79.3 %all-to-all-start.1 = ((bf16[8,308,512]{2,1,0:T(8,128)(2,1)}), bf16[8,308,512]{2,1,0:T(8,128)(2,1)S(1)}, u32[]{:S(2)}, u32[]{:S(2)}) async-start(bf16[8,308,512]{2,1,0:T(8,128)(2,1)} %reshape.293), calls=%async_computation.1 | async-start | bytes 5111808 | tf_op jit(solution)/shard_map/all_to_all | solution.py:46
  218.7 178.6 %all-gather.19.cloned.1.call-start = ((), (), s32[]{:S(2)}) async-start(), calls=%async_computation.11 | async-start | bytes 2621440 | tf_op jit(solution)/shard_map/all_gather | solution.py:110
  231.8 20.5 %collective-permute-start.7 = (bf16[3,64,512]{2,1,0:T(8,128)(2,1)S(1)}, bf16[3,64,512]{2,1,0:T(8,128)(2,1)S(1)}, u32[]{:S(2)}, u32[]{:S(2)}) collective-permute-start(bf16[3,64,512]{2,1,0:T(8,128)(2,1)S(1)} %bitcast.250), channel_id=1, source_target_pairs={{0,4},{4,8},{8,12},{12,16},{16,20},{20,24},{24,28},{28,0},{1,5},{5... | collective-permute-start | bytes 589832 | tf_op jit(solution)/shard_map/ppermute | solution.py:16
  252.4 8.4 collective-permute-start.8
  252.5 20.6 %collective-permute-start.11 = (bf16[3,64,512]{2,1,0:T(8,128)(2,1)S(1)}, bf16[3,64,512]{2,1,0:T(8,128)(2,1)S(1)}, u32[]{:S(2)}, u32[]{:S(2)}) collective-permute-start(bf16[3,64,512]{2,1,0:T(8,128)(2,1)S(1)} %bitcast.251), channel_id=1, source_target_pairs={{0,28},{4,0},{8,4},{12,8},{16,12},{20,16},{24,20},{28,24},{1,29},{... | collective-permute-start | bytes 589832 | tf_op jit(solution)/shard_map/ppermute | solution.py:18
  260.7 12.5 %collective-permute-start.9 = (bf16[3,64,512]{2,1,0:T(8,128)(2,1)}, bf16[3,64,512]{2,1,0:T(8,128)(2,1)}, u32[]{:S(2)}, u32[]{:S(2)}) collective-permute-start(bf16[3,64,512]{2,1,0:T(8,128)(2,1)} %collective-permute-done.8), channel_id=1, source_target_pairs={{0,4},{4,8},{8,12},{12,16},{16,20},{20,24},{24,28},{28,0},{1,5},{5... | collective-permute-start | bytes 589832 | tf_op jit(solution)/shard_map/ppermute | solution.py:16
  273.2 15.2 %collective-permute-start.12 = (bf16[3,64,512]{2,1,0:T(8,128)(2,1)S(1)}, bf16[3,64,512]{2,1,0:T(8,128)(2,1)S(1)}, u32[]{:S(2)}, u32[]{:S(2)}) collective-permute-start(bf16[3,64,512]{2,1,0:T(8,128)(2,1)S(1)} %collective-permute-done.11), channel_id=1, source_target_pairs={{0,28},{4,0},{8,4},{12,8},{16,12},{20,16},{24,20},{28,24},{1,29},{... | collective-permute-start | bytes 589832 | tf_op jit(solution)/shard_map/ppermute | solution.py:18
  273.2 16.7 %collective-permute-start.10 = (bf16[3,64,512]{2,1,0:T(8,128)(2,1)}, bf16[3,64,512]{2,1,0:T(8,128)(2,1)S(1)}, u32[]{:S(2)}, u32[]{:S(2)}) collective-permute-start(bf16[3,64,512]{2,1,0:T(8,128)(2,1)} %collective-permute-done.9), channel_id=1, source_target_pairs={{0,4},{4,8},{8,12},{12,16},{16,20},{20,24},{24,28},{28,0},{1,5},{5... | collective-permute-start | bytes 589832 | tf_op jit(solution)/shard_map/ppermute | solution.py:16
  356.7 36.5 %all-to-all-start.2 = ((bf16[8,308,512]{2,1,0:T(8,128)(2,1)}), bf16[8,308,512]{2,1,0:T(8,128)(2,1)}, u32[]{:S(2)}, u32[]{:S(2)}) async-start(bf16[8,308,512]{2,1,0:T(8,128)(2,1)} %reshape.296), calls=%async_computation.2 | async-start | bytes 5111808 | tf_op jit(solution)/shard_map/all_to_all | solution.py:46
  361.2 49.8 %all-gather.21.cloned.1.call-start = ((), (), s32[]{:S(2)}) async-start(), calls=%async_computation.12 | async-start | bytes 2621440 | tf_op jit(solution)/shard_map/all_gather | solution.py:115
  426.0 36.1 %all-to-all-start.3 = ((bf16[8,308,512]{2,1,0:T(8,128)(2,1)}), bf16[8,308,512]{2,1,0:T(8,128)(2,1)}, u32[]{:S(2)}, u32[]{:S(2)}) async-start(bf16[8,308,512]{2,1,0:T(8,128)(2,1)} %reshape.298), calls=%async_computation.3 | async-start | bytes 5111808 | tf_op jit(solution)/shard_map/all_to_all | solution.py:46
  559.5 36.4 %all-to-all-start.5 = ((bf16[8,308,512]{2,1,0:T(8,128)(2,1)}), bf16[8,308,512]{2,1,0:T(8,128)(2,1)}, u32[]{:S(2)}, u32[]{:S(2)}) async-start(bf16[8,308,512]{2,1,0:T(8,128)(2,1)} %reshape.302), calls=%async_computation.5 | async-start | bytes 5111808 | tf_op jit(solution)/shard_map/all_to_all | solution.py:46
  673.0 36.1 %all-to-all-start.6 = ((bf16[8,308,512]{2,1,0:T(8,128)(2,1)}), bf16[8,308,512]{2,1,0:T(8,128)(2,1)}, u32[]{:S(2)}, u32[]{:S(2)}) async-start(bf16[8,308,512]{2,1,0:T(8,128)(2,1)} %reshape.305), calls=%async_computation.6 | async-start | bytes 5111808 | tf_op jit(solution)/shard_map/all_to_all | solution.py:46
  743.4 70.6 %all-to-all-start.7 = ((bf16[8,308,512]{2,1,0:T(8,128)(2,1)}), bf16[8,308,512]{2,1,0:T(8,128)(2,1)}, u32[]{:S(2)}, u32[]{:S(2)}) async-start(bf16[8,308,512]{2,1,0:T(8,128)(2,1)} %reshape.307), calls=%async_computation.7 | async-start | bytes 5111808 | tf_op jit(solution)/shard_map/all_to_all | solution.py:46
  747.9 155.5 %reduce-scatter.4.cloned.1.call-start = ((), (), s32[]{:S(2)}) async-start(), calls=%async_computation.13 | async-start | bytes 294912
  871.8 96.7 %all-reduce.6.cloned.1.call-start = ((), (), s32[]{:S(2)}) async-start(), calls=%async_computation.14 | async-start | bytes 4194304
  (141 other events, 1494.8 us)
Sparse Core Ops, SparseCore 0:
  26.5 46.9 all-gather.14
  157.0 45.9 all-gather.16
  260.9 44.9 all-gather.18
  363.2 44.9 all-gather.20
  871.9 31.4 reduce-scatter.3
  906.6 61.8 all-reduce.5
